TPU v7x, 32 devices: a whole 2x2x4 slice. The times are simulated.
32 devices in a mesh: img: 8 (over z, y), txt: 4 (over x, core).
Axes of the slice: x: 2, y: 2, z: 4, core: 2. Of those that a mesh axis runs over, the one named last changes fastest.
Arguments:
- images: float32 [1024, 1024], P(('img', 'txt')), may hold values from -1 to 1
- texts: float32 [1024, 1024], P(('txt', 'img')), may hold values from -1 to 1
- labels: int32 [1024], P('img'), may hold values from 0 to 1023, each once
Outputs:
- row_loss: float32 [1024], P('img')
- image_grad: float32 [1024, 1024], P(('img', 'txt'))
- text_grad: float32 [1024, 1024], P(('txt', 'img'))
Inputs may be any that keep to these rules, and one draw needn't show every extreme that they name: `labels`: each text index appears exactly once.
All inputs are finite; a program needn't handle non-finite values.
Results may differ from a plain program's by a relative error of at most 0.017.
Values may be sent and summed in bfloat16 or wider, within the bound.
A program may use at most 64 MiB of HBM per device.

v0:
```python
import jax
import jax.numpy as jnp
from jax import lax
from jax.sharding import PartitionSpec as P

logit_scale = 100.0


def merged(part, axis, combine):
    gathered = jax.tree.map(lambda a: lax.all_gather(a, axis), part)

    def take(source):
        return jax.tree.map(lambda a: lax.dynamic_index_in_dim(a, source, 0, False), gathered)

    return lax.fori_loop(
        1, lax.axis_size(axis), lambda source, state: combine(state, take(source)), take(0)
    )


def combine(earlier, later):
    highest = jnp.maximum(earlier[0], later[0])
    total = earlier[1] * jnp.exp(earlier[0] - highest) + later[1] * jnp.exp(later[0] - highest)
    return (highest, total, earlier[2] + later[2])


def local(images, texts, labels):
    img_panel = lax.all_gather(images.astype(jnp.bfloat16), "txt", axis=0, tiled=True)
    txt_panel = lax.all_gather(texts.astype(jnp.bfloat16), "img", axis=0, tiled=True)
    text_rows = txt_panel.shape[0]
    logits = logit_scale * lax.dot_general(
        img_panel, txt_panel, (((1,), (1,)), ((), ())), preferred_element_type=jnp.float32
    )
    columns = lax.axis_index("txt") * text_rows + lax.broadcasted_iota(jnp.int32, (1, text_rows), 1)
    hits = columns == labels[:, None]
    highest = jnp.max(logits, axis=1)
    exp_total = jnp.sum(jnp.exp(logits - highest[:, None]), axis=1)
    positive = jnp.sum(jnp.where(hits, logits, 0.0), axis=1)
    highest, exp_total, positive = merged((highest, exp_total, positive), "txt", combine)
    log_total = highest + jnp.log(exp_total)
    row_loss = log_total - positive
    grad_tile = (
        logit_scale * (jnp.exp(logits - log_total[:, None]) - hits.astype(jnp.float32))
    ).astype(jnp.bfloat16)
    terms = jnp.dot(grad_tile, txt_panel, preferred_element_type=jnp.float32)
    image_grad = lax.psum_scatter(
        terms.astype(jnp.bfloat16), "txt", scatter_dimension=0, tiled=True
    ).astype(jnp.float32)
    terms = lax.dot_general(
        grad_tile, img_panel, (((0,), (0,)), ((), ())), preferred_element_type=jnp.float32
    )
    text_grad = lax.psum_scatter(
        terms.astype(jnp.bfloat16), "img", scatter_dimension=0, tiled=True
    ).astype(jnp.float32)
    return (row_loss, image_grad, text_grad)


def solution(mesh):
    in_specs = (P(("img", "txt"), None), P(("txt", "img"), None), P("img"))
    out_specs = (P("img"), P(("img", "txt"), None), P(("txt", "img"), None))
    return jax.shard_map(local, mesh=mesh, in_specs=in_specs, out_specs=out_specs, check_vma=False)
```

profile of v0, /device:TPU:0, one launch (start us, length us, event | category | flops | bytes accessed | tf_op | source)
XLA Modules:
  0.0 161.3 jit_solution(13547509192258138272)
XLA Ops:
  7.2 0.0 reduce-scatter.3.cloned.1.call-start
  7.2 0.9 convert_element_type.24
  8.1 0.0 copy-start
  8.1 7.4 %all_gather.24 = bf16[128,1024]{1,0:T(8,128)(2,1)S(1)} all-gather(bf16[32,1024]{1,0:T(8,128)(2,1)S(1)} %convert_element_type.24), channel_id=1, replica_groups=mesh['img'=8,'txt'=4] {'txt'}, dimensions={0}, use_global_device_ids=true | all-gather | bytes 327680 | tf_op jit(solution)/shard_map/all_gather | solution.py:27
  15.5 0.0 copy-done
  15.5 31.9 %all_gather.25 = bf16[256,1024]{1,0:T(8,128)(2,1)S(1)} all-gather(bf16[32,1024]{1,0:T(8,128)(2,1)S(1)} %convert_element_type.25), channel_id=1, replica_groups=mesh['img'=8,'txt'=4] {'img'}, dimensions={0}, use_global_device_ids=true | all-gather | bytes 589824 | tf_op jit(solution)/shard_map/all_gather | solution.py:28
  47.4 0.4 fusion.15
  47.8 5.1 %all-gather.3 = f32[4,1,128]{2,1,0:T(1,128)S(1)} all-gather(f32[1,1,128]{2,1,0:T(1,128)S(1)} %bitcast.38), channel_id=2, replica_groups=mesh['img'=8,'txt'=4] {'txt'}, dimensions={0}, use_global_device_ids=true | all-gather | bytes 2560 | tf_op jit(solution)/shard_map/all_gather | solution.py:10
  52.9 0.0 copy-start.1
  52.9 0.7 copy-done.1
  53.6 0.2 fusion.7
  53.7 5.1 %all-gather.4 = f32[4,1,128]{2,1,0:T(1,128)S(1)} all-gather(f32[1,1,128]{2,1,0:T(1,128)S(1)} %bitcast.40), channel_id=3, replica_groups=mesh['img'=8,'txt'=4] {'txt'}, dimensions={0}, use_global_device_ids=true | all-gather | bytes 2560 | tf_op jit(solution)/shard_map/all_gather | solution.py:10
  58.8 5.0 %all-gather.5 = f32[4,1,128]{2,1,0:T(1,128)S(1)} all-gather(f32[1,1,128]{2,1,0:T(1,128)S(1)} %bitcast.39), channel_id=4, replica_groups=mesh['img'=8,'txt'=4] {'txt'}, dimensions={0}, use_global_device_ids=true | all-gather | bytes 2560 | tf_op jit(solution)/shard_map/all_gather | solution.py:10
  63.9 0.1 while.19
  64.0 0.5 fusion.14
  64.5 1.0 convolution_convert_fusion.1
  65.5 0.0 reduce-scatter.3.cloned.1.call-update
  65.5 0.0 reduce-scatter.5.cloned.1.call-start
  65.6 1.2 convolution_convert_fusion
  66.8 0.0 reduce-scatter.5.cloned.1.call-update
  66.8 19.7 %reduce-scatter.3.cloned.1.call-done = bf16[32,1024]{1,0:T(8,128)(2,1)} async-done(((bf16[128,1024]{1,0:T(8,128)(2,1)}), bf16[32,1024]{1,0:T(8,128)(2,1)}) %reduce-scatter.3.cloned.1.call-update) | async-done | bytes 65552 | tf_op jit(solution)/shard_map/reduce_scatter | solution.py:45
  86.5 1.5 convert_element_type.29
  88.0 65.0 %reduce-scatter.5.cloned.1.call-done = bf16[32,1024]{1,0:T(8,128)(2,1)} async-done(((bf16[256,1024]{1,0:T(8,128)(2,1)}), bf16[32,1024]{1,0:T(8,128)(2,1)}) %reduce-scatter.5.cloned.1.call-update) | async-done | bytes 65552 | tf_op jit(solution)/shard_map/reduce_scatter | solution.py:51
  152.9 1.5 convert_element_type.31
  (8 shorter events, 0.1 us)
Async XLA Ops:
  7.2 79.3 %reduce-scatter.3.cloned.1.call-start = ((), (), s32[]{:S(2)}) async-start(), calls=%async_computation.2 | async-start | bytes 327680 | tf_op jit(solution)/shard_map/reduce_scatter | solution.py:45
  8.1 7.4 %copy-start = (f32[32,1024]{1,0:T(8,128)S(1)}, f32[32,1024]{1,0:T(8,128)}, u32[]{:S(2)}) copy-start(f32[32,1024]{1,0:T(8,128)} %param.6) | copy-start | bytes 393220
  52.9 0.7 copy-start.1
  65.5 87.4 %reduce-scatter.5.cloned.1.call-start = ((), (), s32[]{:S(2)}) async-start(), calls=%async_computation.3 | async-start | bytes 589824 | tf_op jit(solution)/shard_map/reduce_scatter | solution.py:51
Sparse Core Ops, SparseCore 0:
  65.6 20.7 reduce-scatter.2
  89.8 63.0 reduce-scatter.4
where the time goes:
time: 162 us; the launch traced here: 161 us
  waiting for transfers between devices  84.7 us (52%)
  blocking collectives  54.5 us (34%)
  between operations  14.1 us (9%)
  other arithmetic  4.71 us (3%)
  matrix products  2.58 us (2%)
    reduce_scatter x1, waiting for transfers between devices, local(): lax.psum_scatter(terms.astype(jnp.bfloat16), 'img', scatter_dimension=0,...  65 us
    all_gather x1, blocking collectives, local(): lax.all_gather(texts.astype(jnp.bfloat16), 'img', axis=0, tiled=True)  31.9 us
    reduce_scatter x1, waiting for transfers between devices, local(): lax.psum_scatter(terms.astype(jnp.bfloat16), 'txt', scatter_dimension=0,...  19.7 us
    all_gather x3, blocking collectives, merged(): gathered = jax.tree.map(lambda a: lax.all_gather(a, axis), part)  15.2 us
    all_gather x1, blocking collectives, local(): lax.all_gather(images.astype(jnp.bfloat16), 'txt', axis=0, tiled=True)  7.35 us
  transfers between devices with their start and end apart: 2, of which 2 were waited for; matrix products, arithmetic and copies ran while one was open for 2% of the time, Pallas kernels for 0%

commit v1 on v0

--- a/solution.py
+++ b/solution.py
@@ -25,7 +25,17 @@
 
 def local(images, texts, labels):
     img_panel = lax.all_gather(images.astype(jnp.bfloat16), "txt", axis=0, tiled=True)
-    txt_panel = lax.all_gather(texts.astype(jnp.bfloat16), "img", axis=0, tiled=True)
+    array = texts.astype(jnp.bfloat16)
+    ways = lax.axis_size("img")
+    up = [(d, (d + 1) % ways) for d in range(ways)]
+    down = [(d, (d - 1) % ways) for d in range(ways)]
+    earlier_2, later_2 = ([array], [array])
+    for _ in range(ways // 2):
+        earlier_2.append(lax.ppermute(earlier_2[-1], "img", up))
+    for _ in range((ways - 1) // 2):
+        later_2.append(lax.ppermute(later_2[-1], "img", down))
+    line = jnp.concatenate([*earlier_2[::-1], *later_2[1:]], axis=0)
+    txt_panel = jnp.roll(line, (lax.axis_index("img") - ways // 2) * array.shape[0], axis=0)
     text_rows = txt_panel.shape[0]
     logits = logit_scale * lax.dot_general(
         img_panel, txt_panel, (((1,), (1,)), ((), ())), preferred_element_type=jnp.float32

time: 162 us -> 158 us (0.975)
  blocking collectives: 54.5 us -> 21 us
  starting transfers between devices: 0.08 us -> 17.3 us
  waiting for transfers between devices: 84.7 us -> 96.1 us
    all_gather x1 -> x0, blocking collectives: 31.9 us -> none  [local(): lax.all_gather(texts.astype(jnp.bfloat16), 'img', axis=0, tiled=True)]
    ppermute x0 -> x7, starting transfers between devices: none -> 17.2 us  [the longest x3 14.2 us: local(): later_2.append(lax.ppermute(later_2[-1], 'img', down))]
    ppermute x0 -> x7, waiting for transfers between devices: none -> 10.7 us  [the longest x4 9.73 us: local(): earlier_2.append(lax.ppermute(earlier_2[-1], 'img', up))]
  transfers between devices with their start and end apart: 2 -> 9, of which waited for: 2 -> 6; matrix products, arithmetic and copies ran while one was open for 2% -> 2% of each run, Pallas kernels for 0% -> 0%
where the time goes in v1:
time: 158 us; the launch traced here: 157 us
  waiting for transfers between devices  96.1 us (61%)
  blocking collectives  21 us (13%)
  starting transfers between devices  17.3 us (11%)
  between operations  14.2 us (9%)
  other arithmetic  4.7 us (3%)
  matrix products  2.5 us (2%)
  local copies, waits for them, and re-layouts  1.63 us (1%)
    reduce_scatter x1, waiting for transfers between devices, local(): lax.psum_scatter(terms.astype(jnp.bfloat16), 'img', scatter_dimension=0,...  64.5 us
    reduce_scatter x1, waiting for transfers between devices, local(): lax.psum_scatter(terms.astype(jnp.bfloat16), 'txt', scatter_dimension=0,...  20.9 us
    all_gather x3, blocking collectives, merged(): gathered = jax.tree.map(lambda a: lax.all_gather(a, axis), part)  15.1 us
    ppermute x3, starting transfers between devices, local(): later_2.append(lax.ppermute(later_2[-1], 'img', down))  14.2 us
    ppermute x4, waiting for transfers between devices, local(): earlier_2.append(lax.ppermute(earlier_2[-1], 'img', up))  9.73 us
    all_gather x1, blocking collectives, local(): lax.all_gather(images.astype(jnp.bfloat16), 'txt', axis=0, tiled=True)  5.89 us
  transfers between devices with their start and end apart: 9, of which 6 were waited for; matrix products, arithmetic and copies ran while one was open for 2% of the time, Pallas kernels for 0%

profile of v1, /device:TPU:0, one launch (start us, length us, event | category | flops | bytes accessed | tf_op | source)
XLA Modules:
  0.0 157.5 jit_solution(17834609707366996570)
XLA Ops:
  7.2 0.9 convert_element_type.24
  8.2 3.0 %collective-permute-start = (bf16[32,1024]{1,0:T(8,128)(2,1)S(1)}, bf16[32,1024]{1,0:T(8,128)(2,1)S(1)}, u32[]{:S(2)}, u32[]{:S(2)}) collective-permute-start(bf16[32,1024]{1,0:T(8,128)(2,1)S(1)} %convert_element_type.24), channel_id=1, source_target_pairs={{0,4},{4,8},{8,12},{12,16},{16,20},{20,24},{24,28},{28,0},{1,5},{5... | collective-permute-start | bytes 196616 | tf_op jit(solution)/shard_map/ppermute | solution.py:34
  11.2 5.3 %collective-permute-done = bf16[32,1024]{1,0:T(8,128)(2,1)S(1)} collective-permute-done((bf16[32,1024]{1,0:T(8,128)(2,1)S(1)}, bf16[32,1024]{1,0:T(8,128)(2,1)S(1)}, u32[]{:S(2)}, u32[]{:S(2)}) %collective-permute-start) | collective-permute-done | bytes 65568 | tf_op jit(solution)/shard_map/ppermute | solution.py:34
  16.5 4.7 %collective-permute-start.4 = (bf16[32,1024]{1,0:T(8,128)(2,1)S(1)}, bf16[32,1024]{1,0:T(8,128)(2,1)S(1)}, u32[]{:S(2)}, u32[]{:S(2)}) collective-permute-start(bf16[32,1024]{1,0:T(8,128)(2,1)S(1)} %convert_element_type.24), channel_id=1, source_target_pairs={{0,28},{4,0},{8,4},{12,8},{16,12},{20,16},{24,20},{28,24},{1,29},{... | collective-permute-start | bytes 196616 | tf_op jit(solution)/shard_map/ppermute | solution.py:36
  21.2 2.2 %collective-permute-done.1 = bf16[32,1024]{1,0:T(8,128)(2,1)S(1)} collective-permute-done((bf16[32,1024]{1,0:T(8,128)(2,1)S(1)}, bf16[32,1024]{1,0:T(8,128)(2,1)S(1)}, u32[]{:S(2)}, u32[]{:S(2)}) %collective-permute-start.1) | collective-permute-done | bytes 65568 | tf_op jit(solution)/shard_map/ppermute | solution.py:34
  23.5 4.7 %collective-permute-start.5 = (bf16[32,1024]{1,0:T(8,128)(2,1)S(1)}, bf16[32,1024]{1,0:T(8,128)(2,1)S(1)}, u32[]{:S(2)}, u32[]{:S(2)}) collective-permute-start(bf16[32,1024]{1,0:T(8,128)(2,1)S(1)} %collective-permute-done.4), channel_id=1, source_target_pairs={{0,28},{4,0},{8,4},{12,8},{16,12},{20,16},{24,20},{28,24},{1,29},{... | collective-permute-start | bytes 196616 | tf_op jit(solution)/shard_map/ppermute | solution.py:36
  28.2 2.2 %collective-permute-done.2 = bf16[32,1024]{1,0:T(8,128)(2,1)S(1)} collective-permute-done((bf16[32,1024]{1,0:T(8,128)(2,1)S(1)}, bf16[32,1024]{1,0:T(8,128)(2,1)S(1)}, u32[]{:S(2)}, u32[]{:S(2)}) %collective-permute-start.2) | collective-permute-done | bytes 65568 | tf_op jit(solution)/shard_map/ppermute | solution.py:34
  30.4 5.9 %all_gather.21 = bf16[128,1024]{1,0:T(8,128)(2,1)S(1)} all-gather(bf16[32,1024]{1,0:T(8,128)(2,1)S(1)} %convert_element_type.25), channel_id=1, replica_groups=mesh['img'=8,'txt'=4] {'txt'}, dimensions={0}, use_global_device_ids=true | all-gather | bytes 327680 | tf_op jit(solution)/shard_map/all_gather | solution.py:27
  36.3 4.7 %collective-permute-start.6 = (bf16[32,1024]{1,0:T(8,128)(2,1)S(1)}, bf16[32,1024]{1,0:T(8,128)(2,1)S(1)}, u32[]{:S(2)}, u32[]{:S(2)}) collective-permute-start(bf16[32,1024]{1,0:T(8,128)(2,1)S(1)} %collective-permute-done.5), channel_id=1, source_target_pairs={{0,28},{4,0},{8,4},{12,8},{16,12},{20,16},{24,20},{28,24},{1,29},{... | collective-permute-start | bytes 196616 | tf_op jit(solution)/shard_map/ppermute | solution.py:36
  41.1 0.9 copy-done
  42.0 0.9 collective-permute-done.6
  43.1 0.3 fusion.22
  43.4 0.7 copy-done.2
  44.0 0.1 fusion.9
  44.2 5.1 %all-gather.5 = f32[4,1,128]{2,1,0:T(1,128)S(1)} all-gather(f32[1,1,128]{2,1,0:T(1,128)S(1)} %bitcast.52), channel_id=4, replica_groups=mesh['img'=8,'txt'=4] {'txt'}, dimensions={0}, use_global_device_ids=true | all-gather | bytes 2560 | tf_op jit(solution)/shard_map/all_gather | solution.py:10
  49.2 5.0 %all-gather.4 = f32[4,1,128]{2,1,0:T(1,128)S(1)} all-gather(f32[1,1,128]{2,1,0:T(1,128)S(1)} %bitcast.51), channel_id=3, replica_groups=mesh['img'=8,'txt'=4] {'txt'}, dimensions={0}, use_global_device_ids=true | all-gather | bytes 2560 | tf_op jit(solution)/shard_map/all_gather | solution.py:10
  54.3 5.0 %all-gather.3 = f32[4,1,128]{2,1,0:T(1,128)S(1)} all-gather(f32[1,1,128]{2,1,0:T(1,128)S(1)} %bitcast.50), channel_id=2, replica_groups=mesh['img'=8,'txt'=4] {'txt'}, dimensions={0}, use_global_device_ids=true | all-gather | bytes 2560 | tf_op jit(solution)/shard_map/all_gather | solution.py:10
  59.4 0.5 fusion.21
  60.0 1.0 convolution_convert_fusion.1
  61.1 1.1 convolution_convert_fusion
  62.2 20.9 %reduce-scatter.3.cloned.1.call-done = bf16[32,1024]{1,0:T(8,128)(2,1)} async-done(((bf16[128,1024]{1,0:T(8,128)(2,1)}), bf16[32,1024]{1,0:T(8,128)(2,1)}) %reduce-scatter.3.cloned.1.call-update) | async-done | bytes 65552 | tf_op jit(solution)/shard_map/reduce_scatter | solution.py:55
  83.1 1.5 convert_element_type.29
  84.6 64.5 %reduce-scatter.5.cloned.1.call-done = bf16[32,1024]{1,0:T(8,128)(2,1)} async-done(((bf16[256,1024]{1,0:T(8,128)(2,1)}), bf16[32,1024]{1,0:T(8,128)(2,1)}) %reduce-scatter.5.cloned.1.call-update) | async-done | bytes 65552 | tf_op jit(solution)/shard_map/reduce_scatter | solution.py:61
  149.1 1.5 convert_element_type.31
  (39 shorter events, 0.5 us)
Async XLA Ops:
  7.2 14.1 %copy-start.1 = (f32[32,1024]{1,0:T(8,128)S(1)}, f32[32,1024]{1,0:T(8,128)}, u32[]{:S(2)}) copy-start(f32[32,1024]{1,0:T(8,128)} %param.5) | copy-start | bytes 393220
  7.2 75.9 %reduce-scatter.3.cloned.1.call-start = ((), (), s32[]{:S(2)}) async-start(), calls=%async_computation.2 | async-start | bytes 327680 | tf_op jit(solution)/shard_map/reduce_scatter | solution.py:55
  8.2 8.3 %collective-permute-start = (bf16[32,1024]{1,0:T(8,128)(2,1)S(1)}, bf16[32,1024]{1,0:T(8,128)(2,1)S(1)}, u32[]{:S(2)}, u32[]{:S(2)}) collective-permute-start(bf16[32,1024]{1,0:T(8,128)(2,1)S(1)} %convert_element_type.24), channel_id=1, source_target_pairs={{0,4},{4,8},{8,12},{12,16},{16,20},{20,24},{24,28},{28,0},{1,5},{5... | collective-permute-start | bytes 196616 | tf_op jit(solution)/shard_map/ppermute | solution.py:34
  16.5 7.0 %collective-permute-start.1 = (bf16[32,1024]{1,0:T(8,128)(2,1)S(1)}, bf16[32,1024]{1,0:T(8,128)(2,1)S(1)}, u32[]{:S(2)}, u32[]{:S(2)}) collective-permute-start(bf16[32,1024]{1,0:T(8,128)(2,1)S(1)} %collective-permute-done), channel_id=1, source_target_pairs={{0,4},{4,8},{8,12},{12,16},{16,20},{20,24},{24,28},{28,0},{1,5},{5... | collective-permute-start | bytes 196616 | tf_op jit(solution)/shard_map/ppermute | solution.py:34
  16.5 7.0 %collective-permute-start.4 = (bf16[32,1024]{1,0:T(8,128)(2,1)S(1)}, bf16[32,1024]{1,0:T(8,128)(2,1)S(1)}, u32[]{:S(2)}, u32[]{:S(2)}) collective-permute-start(bf16[32,1024]{1,0:T(8,128)(2,1)S(1)} %convert_element_type.24), channel_id=1, source_target_pairs={{0,28},{4,0},{8,4},{12,8},{16,12},{20,16},{24,20},{28,24},{1,29},{... | collective-permute-start | bytes 196616 | tf_op jit(solution)/shard_map/ppermute | solution.py:36
  23.5 7.0 %collective-permute-start.2 = (bf16[32,1024]{1,0:T(8,128)(2,1)S(1)}, bf16[32,1024]{1,0:T(8,128)(2,1)S(1)}, u32[]{:S(2)}, u32[]{:S(2)}) collective-permute-start(bf16[32,1024]{1,0:T(8,128)(2,1)S(1)} %collective-permute-done.1), channel_id=1, source_target_pairs={{0,4},{4,8},{8,12},{12,16},{16,20},{20,24},{24,28},{28,0},{1,5},{5... | collective-permute-start | bytes 196616 | tf_op jit(solution)/shard_map/ppermute | solution.py:34
  23.5 12.8 %collective-permute-start.5 = (bf16[32,1024]{1,0:T(8,128)(2,1)S(1)}, bf16[32,1024]{1,0:T(8,128)(2,1)S(1)}, u32[]{:S(2)}, u32[]{:S(2)}) collective-permute-start(bf16[32,1024]{1,0:T(8,128)(2,1)S(1)} %collective-permute-done.4), channel_id=1, source_target_pairs={{0,28},{4,0},{8,4},{12,8},{16,12},{20,16},{24,20},{28,24},{1,29},{... | collective-permute-start | bytes 196616 | tf_op jit(solution)/shard_map/ppermute | solution.py:36
  30.4 10.6 %collective-permute-start.3 = (bf16[32,1024]{1,0:T(8,128)(2,1)S(1)}, bf16[32,1024]{1,0:T(8,128)(2,1)S(1)}, u32[]{:S(2)}, u32[]{:S(2)}) collective-permute-start(bf16[32,1024]{1,0:T(8,128)(2,1)S(1)} %collective-permute-done.2), channel_id=1, source_target_pairs={{0,4},{4,8},{8,12},{12,16},{16,20},{20,24},{24,28},{28,0},{1,5},{5... | collective-permute-start | bytes 196616 | tf_op jit(solution)/shard_map/ppermute | solution.py:34
  36.3 6.6 %collective-permute-start.6 = (bf16[32,1024]{1,0:T(8,128)(2,1)S(1)}, bf16[32,1024]{1,0:T(8,128)(2,1)S(1)}, u32[]{:S(2)}, u32[]{:S(2)}) collective-permute-start(bf16[32,1024]{1,0:T(8,128)(2,1)S(1)} %collective-permute-done.5), channel_id=1, source_target_pairs={{0,28},{4,0},{8,4},{12,8},{16,12},{20,16},{24,20},{28,24},{1,29},{... | collective-permute-start | bytes 196616 | tf_op jit(solution)/shard_map/ppermute | solution.py:36
  41.1 0.9 copy-start
  43.4 0.7 copy-start.2
  61.0 88.1 %reduce-scatter.5.cloned.1.call-start = ((), (), s32[]{:S(2)}) async-start(), calls=%async_computation.3 | async-start | bytes 589824 | tf_op jit(solution)/shard_map/reduce_scatter | solution.py:61
Sparse Core Ops, SparseCore 0:
  61.1 21.9 reduce-scatter.2
  86.4 62.6 reduce-scatter.4
